TPU v7x, 32 devices: a whole 2x2x4 slice. The times are simulated.
32 devices in a mesh: groups: 1, wide: 16 (over z, y, core), tp: 2 (over x), sub: 1.
Axes of the slice: x: 2, y: 2, z: 4, core: 2. Of those that a mesh axis runs over, the one named last changes fastest.
Arguments:
- moe_input: bfloat16 [128, 3584], P(('groups', 'wide', 'tp', 'sub')), may hold values from -6 to 6
- routes: int32 [128, 8], P(('groups', 'wide', 'tp', 'sub')), may hold values from 0 to 15, all different within a row; in each aligned block of 4 rows (0 to 3, 4 to 7, ...) at most 4 rows name the same one
- router_weight: bfloat16 [3584, 16], replicated, may hold values from -0.1875 to 0.1875
- gate_weight: bfloat16 [16, 3584, 1024], P('wide', None, ('tp', 'sub')), may hold values from -0.09375 to 0.09375
- up_weight: bfloat16 [16, 3584, 1024], P('wide', None, ('tp', 'sub')), may hold values from -0.09375 to 0.09375
- down_weight: bfloat16 [16, 1024, 3584], P('wide', ('tp', 'sub')), may hold values from -0.1875 to 0.1875
- query_latent: bfloat16 [16, 128, 512], P(('groups', 'wide', 'sub')), may hold values from -20 to 20
- query_rope: bfloat16 [16, 64, 128], P(('groups', 'wide', 'sub')), may hold values from -6 to 6
- cache_latent: bfloat16 [16, 4096, 512], P(('groups', 'wide', 'sub'), 'tp'), may hold values from -6 to 6
- cache_rope: bfloat16 [16, 64, 4096], P(('groups', 'wide', 'sub'), None, 'tp'), may hold values from -6 to 6
- cache_lengths: int32 [16], P(('groups', 'wide', 'sub')), may hold values from 256 to 4096, as said below
Outputs:
- moe_out: bfloat16 [128, 3584], P(('groups', 'wide', 'tp', 'sub'))
- att_out: bfloat16 [16, 128, 512], P(('groups', 'wide', 'sub'))
Inputs may be any that keep to these rules, and one draw needn't show every extreme that they name: `routes`: within the 4 rows of one device no expert is named by more than 4 rows, and in some device's rows an expert is named by exactly 4 of them. Row r attends to its cached positions 0 to cache_lengths[r] - 1; in every draw some row has exactly 4096.
All inputs are finite; a program needn't handle non-finite values.
Results may differ from a plain program's by a relative error of at most 0.015.
Values may be sent and summed in bfloat16 or wider, within the bound.
No kernel may reach another device: no remote copies, remote signals or barrier semaphores. Data moves between devices by JAX's collectives and lax.ppermute only.
A program may use at most 64 MiB of HBM per device.

v0:
```python
import jax
import jax.numpy as jnp
from jax import lax
from jax.sharding import PartitionSpec as P

score_scale = 0.07216878364870323
route_scale = 2.5


def slot_tables(route_block, experts, capacity):
    entries, picks = route_block.shape
    flattened = route_block.reshape(entries * picks)
    expert_ids = jnp.arange(experts, dtype=jnp.int32)
    onehot = (flattened[:, None] == expert_ids[None, :]).astype(jnp.int32)
    earlier = jnp.cumsum(onehot, axis=0) - onehot
    position = jnp.sum(earlier * onehot, axis=1)
    target = flattened * capacity + position
    slot_ids = jnp.arange(experts * capacity, dtype=jnp.int32)
    select = (target[:, None] == slot_ids[None, :]).astype(jnp.float32)
    return (
        select.reshape(entries, picks, experts * capacity),
        onehot.reshape(entries, picks, experts).astype(jnp.float32),
    )


def expert_part(row_block, gate_slice, up_slice, down_slice):
    gate_value = jnp.dot(row_block, gate_slice, preferred_element_type=jnp.float32)
    up_value = jnp.dot(row_block, up_slice, preferred_element_type=jnp.float32)
    hidden = (jax.nn.silu(gate_value) * up_value).astype(jnp.bfloat16)
    return jnp.dot(hidden, down_slice, preferred_element_type=jnp.float32).astype(jnp.bfloat16)


def body(
    moe_input,
    routes,
    router_weight,
    gate_weight,
    up_weight,
    down_weight,
    query_latent,
    query_rope,
    cache_latent,
    cache_rope,
    cache_lengths,
):
    experts = lax.axis_size("wide") * gate_weight.shape[0]
    row_count, picks = routes.shape
    width = moe_input.shape[1]
    capacity = min(row_count, max(2, 2 * row_count * picks // experts))
    select, picked = slot_tables(routes, experts, capacity)
    logits = jnp.dot(moe_input, router_weight, preferred_element_type=jnp.float32)
    probs = jax.nn.sigmoid(logits)
    chosen = jnp.sum(picked * probs[:, None, :], axis=2)
    gates = route_scale * chosen / jnp.sum(chosen, axis=1, keepdims=True)
    spread_rows = jnp.sum(select, axis=1).T.astype(jnp.bfloat16)
    weighting = jnp.sum(gates[:, :, None] * select, axis=1)
    gate_slice = gate_weight[0]
    up_slice = up_weight[0]
    down_slice = down_weight[0]
    packed = jnp.dot(spread_rows, moe_input, preferred_element_type=jnp.float32)
    packed = packed.astype(jnp.bfloat16).reshape(experts, capacity, width)
    arrived = lax.all_to_all(packed, "wide", split_axis=0, concat_axis=0, tiled=True)
    column = lax.all_gather(arrived, ("tp", "sub"), axis=0, tiled=True)
    flattened = column.reshape(-1, width)
    summed = lax.psum_scatter(
        expert_part(flattened, gate_slice, up_slice, down_slice)
        .astype(jnp.float32)
        .astype(jnp.bfloat16),
        ("tp", "sub"),
        scatter_dimension=0,
        tiled=True,
    )
    own_out = summed.reshape(arrived.shape[0], capacity, width)
    returned = lax.all_to_all(own_out, "wide", split_axis=0, concat_axis=0, tiled=True)
    outputs = returned.reshape(experts * capacity, width)
    combined = jnp.dot(weighting, outputs.astype(jnp.float32), precision=lax.Precision.HIGHEST)
    moe_out = combined.astype(jnp.bfloat16)
    local_len = cache_latent.shape[1]
    positions = lax.axis_index("tp") * local_len + jnp.arange(local_len, dtype=jnp.int32)
    scores = jnp.einsum(
        "rhc,rlc->rhl", query_latent, cache_latent, preferred_element_type=jnp.float32
    )
    scores = (
        scores
        + jnp.einsum("rkh,rkl->rhl", query_rope, cache_rope, preferred_element_type=jnp.float32)
    ) * score_scale
    live = positions[None, None, :] < cache_lengths[:, None, None]
    masked = jnp.where(live, scores, -1e30)
    peak = lax.pmax(jnp.max(masked, axis=2), "tp")
    weights = jnp.where(live, jnp.exp(masked - peak[:, :, None]), 0.0)
    denom = jnp.sum(weights, axis=2)
    mixed = jnp.einsum(
        "rhl,rlc->rhc",
        weights.astype(jnp.bfloat16),
        cache_latent,
        preferred_element_type=jnp.float32,
    )
    mixed, denom = (
        lax.psum(mixed.astype(jnp.bfloat16), "tp").astype(jnp.float32),
        lax.psum(denom.astype(jnp.bfloat16), "tp").astype(jnp.float32),
    )
    att_out = (mixed / denom[:, :, None]).astype(jnp.bfloat16)
    return (moe_out, att_out)


def solution(mesh):
    in_specs = (
        P(("groups", "wide", "tp", "sub"), None),
        P(("groups", "wide", "tp", "sub"), None),
        P(),
        P("wide", None, ("tp", "sub")),
        P("wide", None, ("tp", "sub")),
        P("wide", ("tp", "sub"), None),
        P(("groups", "wide", "sub"), None, None),
        P(("groups", "wide", "sub"), None, None),
        P(("groups", "wide", "sub"), "tp", None),
        P(("groups", "wide", "sub"), None, "tp"),
        P(("groups", "wide", "sub")),
    )
    out_specs = (P(("groups", "wide", "tp", "sub"), None), P(("groups", "wide", "sub"), None, None))
    return jax.shard_map(body, mesh=mesh, in_specs=in_specs, out_specs=out_specs, check_vma=False)
```

profile of v0, /device:TPU:0, one launch (start us, length us, event | category | flops | bytes accessed | tf_op | source)
XLA Modules:
  0.0 122.5 jit_solution(11289063658092021254)
XLA Ops:
  7.2 0.0 copy-start
  7.2 0.0 reduce-scatter.2.cloned.1.call-start
  7.2 0.9 eq.36
  8.1 0.1 fusion.45
  8.2 0.1 reduce_window_sum.11
  8.3 0.2 select_reduce_fusion.1
  8.4 0.1 reduce_sum.57
  8.5 0.7 multiply_add_fusion
  9.2 1.1 fusion.25
  10.3 0.9 fusion.43
  11.2 0.1 multiply_divide_fusion
  11.2 0.1 convert_reduce_fusion
  11.3 1.1 convolution_convert_fusion.1
  12.4 0.1 reshape.119
  12.5 20.4 %all_to_all.10 = bf16[16,4,3584]{2,1,0:T(4,128)(2,1)S(1)} all-to-all(bf16[16,4,3584]{2,1,0:T(4,128)(2,1)S(1)} %reshape.119), channel_id=1, replica_groups=mesh['groups'=1,'wide'=16,'tp'=2,'sub'=1] {'wide'}, dimensions={0} | all-to-all | bytes 917504 | tf_op jit(solution)/shard_map/all_to_all | solution.py:62
  33.0 13.3 %all_gather.3 = bf16[32,4,3584]{2,1,0:T(4,128)(2,1)} all-gather(bf16[16,4,3584]{2,1,0:T(4,128)(2,1)S(1)} %all_to_all.10), channel_id=1, replica_groups=mesh['groups'=1,'wide'=16,'tp'=2,'sub'=1] {'tp','sub'}, dimensions={0}, use_global_device_ids=true | all-gather | bytes 1376256 | tf_op jit(solution)/shard_map/all_gather | solution.py:63
  46.3 1.7 %reshape.120 = bf16[128,3584]{1,0:T(8,128)(2,1)S(1)} reshape(bf16[32,4,3584]{2,1,0:T(4,128)(2,1)} %all_gather.3) | data formatting | bytes 1835008 | tf_op jit(solution)/shard_map/reshape | solution.py:64
  47.9 2.7 %fusion.3 = f32[128,512]{1,0:T(8,128)S(1)} fusion(bf16[128,3584]{1,0:T(8,128)(2,1)S(1)} %reshape.120, bf16[1,3584,512]{2,1,0:T(8,128)(2,1)} %param.14), kind=kOutput, calls=%fused_computation.6 | convolution fusion | flops 469762048 | bytes 4849664 | tf_op jit(solution)/shard_map/dot_general | solution.py:27
  50.6 0.0 copy-start.2
  50.6 5.4 %convolution_convert_fusion = bf16[128,3584]{1,0:T(8,128)(2,1)} fusion(bf16[1,512,3584]{2,1,0:T(8,128)(2,1)} %param.16, bf16[128,3584]{1,0:T(8,128)(2,1)S(1)} %reshape.120, bf16[1,3584,512]{2,1,0:T(8,128)(2,1)} %param.15, f32[128,512]{1,0:T(8,128)S(1)} %fusion.3), kind=kOutput, calls=%fused_computation | convolution fusion | flops 940376064 | bytes 9437184 | tf_op jit(solution)/shard_map/dot_general | solution.py:30
  56.0 0.0 copy-start.1
  56.0 0.0 reduce-scatter.2.cloned.1.call-update
  56.7 0.0 copy-done
  56.8 0.0 copy-done.2
  56.8 1.8 %fusion.9 = f32[128,2048]{1,0:T(8,128)} fusion(bf16[1,2048,512]{2,1,0:T(8,128)(2,1)S(1)} %copy-done, bf16[1,128,512]{2,1,0:T(8,128)(2,1)S(1)} %copy-done.2), kind=kOutput, calls=%fused_computation.13 | convolution fusion | flops 268435456 | bytes 3276800 | tf_op jit(solution)/shard_map/rhc,rlc->rhl/dot_general | solution.py:80
  58.6 16.0 %reduce-scatter.2.cloned.1.call-done = bf16[64,3584]{1,0:T(8,128)(2,1)} async-done(((bf16[128,3584]{1,0:T(8,128)(2,1)}), bf16[64,3584]{1,0:T(8,128)(2,1)}) %reduce-scatter.2.cloned.1.call-update) | async-done | bytes 458768 | tf_op jit(solution)/shard_map/reduce_scatter | solution.py:65
  74.5 1.9 %reshape.121 = bf16[16,4,3584]{2,1,0:T(4,128)(2,1)} reshape(bf16[64,3584]{1,0:T(8,128)(2,1)} %reduce-scatter.2.cloned.1.call-done) | data formatting | bytes 917504 | tf_op jit(solution)/shard_map/reshape | solution.py:73
  76.4 5.7 %all-to-all-start.1 = ((bf16[16,4,3584]{2,1,0:T(4,128)(2,1)}), bf16[16,4,3584]{2,1,0:T(4,128)(2,1)}, u32[]{:S(2)}, u32[]{:S(2)}) async-start(bf16[16,4,3584]{2,1,0:T(4,128)(2,1)} %reshape.121), calls=%async_computation.2 | async-start | bytes 917504 | tf_op jit(solution)/shard_map/all_to_all | solution.py:74
  82.1 0.0 all-reduce.2.cloned.1.call-start
  82.1 0.0 copy-done.1
  82.2 1.7 %fusion.49 = (f32[128]{0:T(128)S(1)}, f32[128,2048]{1,0:T(8,128)S(1)}) fusion(f32[128,2048]{1,0:T(8,128)} %fusion.9, bf16[1,64,2048]{2,1,0:T(8,128)(2,1)S(1)} %copy-done.1, bf16[1,64,128]{2,1,0:T(8,128)(2,1)} %param.18, pred[2048]{0:T(1024)(128)(4,1)S(1)} %add_compare_fusion), kind=kOutput, calls=%fused_computation.55 | convolution fusion | flops 34602880 | bytes 2378240 | tf_op jit(solution)/shard_map/rkh,rkl->rhl/dot_general | solution.py:85
  83.8 4.9 %pmax.7 = f32[128]{0:T(128)S(1)} all-reduce(f32[128]{0:T(128)S(1)} %get-tuple-element.6), channel_id=1, replica_groups=mesh['groups'=1,'wide'=16,'tp'=2,'sub'=1] {'tp'}, use_global_device_ids=true, to_apply=%region_8.9 | all-reduce | flops 128 | bytes 1024 | tf_op jit(solution)/shard_map/pmax | solution.py:89
  88.8 1.2 fusion.20
  89.9 0.0 all-reduce.2.cloned.1.call-update
  89.9 0.3 fusion.28
  90.3 4.9 %psum.15 = bf16[128]{0:T(256)(128)(2,1)S(1)} all-reduce(bf16[128]{0:T(256)(128)(2,1)S(1)} %fusion.28), channel_id=1, replica_groups=mesh['groups'=1,'wide'=16,'tp'=2,'sub'=1] {'tp'}, use_global_device_ids=true, to_apply=%region_11.12 | all-reduce | flops 128 | bytes 512 | tf_op jit(solution)/shard_map/psum | solution.py:100
  95.2 16.8 %all-reduce.2.cloned.1.call-done = bf16[1,128,512]{2,1,0:T(8,128)(2,1)} async-done(((bf16[1,128,512]{2,1,0:T(8,128)(2,1)}), bf16[1,128,512]{2,1,0:T(8,128)(2,1)}) %all-reduce.2.cloned.1.call-update) | async-done | bytes 131088 | tf_op jit(solution)/shard_map/psum | solution.py:99
  112.0 1.7 %divide_convert_fusion = bf16[1,128,512]{2,1,0:T(8,128)(2,1)} fusion(bf16[1,128,512]{2,1,0:T(8,128)(2,1)} %all-reduce.2.cloned.1.call-done, f32[128]{0:T(128)S(1)} %div.36), kind=kLoop, calls=%fused_computation.30 | loop fusion | flops 196608 | bytes 262656 | tf_op jit(solution)/shard_map/convert_element_type | solution.py:102
  113.6 0.0 all-to-all-done.1
  113.7 1.1 reshape.122
  114.8 0.9 convolution_convert_fusion.2
  (2 shorter events, 0.0 us)
Async XLA Ops:
  7.2 49.6 %copy-start = (bf16[1,2048,512]{2,1,0:T(8,128)(2,1)S(1)}, bf16[1,2048,512]{2,1,0:T(8,128)(2,1)}, u32[]{:S(2)}) copy-start(bf16[1,2048,512]{2,1,0:T(8,128)(2,1)} %param.19) | copy-start | bytes 6291460
  7.2 67.3 %reduce-scatter.2.cloned.1.call-start = ((), (), s32[]{:S(2)}) async-start(), calls=%async_computation.3 | async-start | bytes 1376256 | tf_op jit(solution)/shard_map/reduce_scatter | solution.py:65
  50.6 6.1 %copy-start.2 = (bf16[1,128,512]{2,1,0:T(8,128)(2,1)S(1)}, bf16[1,128,512]{2,1,0:T(8,128)(2,1)}, u32[]{:S(2)}) copy-start(bf16[1,128,512]{2,1,0:T(8,128)(2,1)} %param.17) | copy-start | bytes 393220
  56.0 26.1 %copy-start.1 = (bf16[1,64,2048]{2,1,0:T(8,128)(2,1)S(1)}, bf16[1,64,2048]{2,1,0:T(8,128)(2,1)}, u32[]{:S(2)}) copy-start(bf16[1,64,2048]{2,1,0:T(8,128)(2,1)} %param.20) | copy-start | bytes 786436
  76.4 37.2 %all-to-all-start.1 = ((bf16[16,4,3584]{2,1,0:T(4,128)(2,1)}), bf16[16,4,3584]{2,1,0:T(4,128)(2,1)}, u32[]{:S(2)}, u32[]{:S(2)}) async-start(bf16[16,4,3584]{2,1,0:T(4,128)(2,1)} %reshape.121), calls=%async_computation.2 | async-start | bytes 917504 | tf_op jit(solution)/shard_map/all_to_all | solution.py:74
  82.1 29.9 %all-reduce.2.cloned.1.call-start = ((), (), s32[]{:S(2)}) async-start(), calls=%async_computation.4 | async-start | bytes 262144 | tf_op jit(solution)/shard_map/psum | solution.py:99
Sparse Core Ops, SparseCore 0:
  56.2 18.3 reduce-scatter.1
  90.1 21.8 all-reduce.1
where the time goes:
time: 123 us
  blocking collectives  43.6 us (35%)
  waiting for transfers between devices  32.8 us (27%)
  matrix products  15.7 us (13%)
  between operations  14.8 us (12%)
  local copies, waits for them, and re-layouts  5.8 us (5%)
  starting transfers between devices  5.74 us (5%)
  other arithmetic  4.05 us (3%)
    all_to_all x1, blocking collectives, body(): lax.all_to_all(packed, 'wide', split_axis=0, concat_axis=0, tiled=True)  20.4 us
    psum x1, waiting for transfers between devices, body(): lax.psum(mixed.astype(jnp.bfloat16), 'tp').astype(jnp.float32)  16.8 us
    reduce_scatter x1, waiting for transfers between devices, body(): lax.psum_scatter(expert_part(flattened, gate_slice, up_slice, down_slice)...  16 us
    all_gather x1, blocking collectives, body(): column = lax.all_gather(arrived, ('tp', 'sub'), axis=0, tiled=True)  13.3 us
    all_to_all x1, starting transfers between devices, body(): lax.all_to_all(own_out, 'wide', split_axis=0, concat_axis=0, tiled=True)  5.66 us
    dot_general x1, matrix products, expert_part(): jnp.dot(hidden, down_slice, preferred_element_type=jnp.float32)  5.39 us
    pmax x1, blocking collectives, body(): peak = lax.pmax(jnp.max(masked, axis=2), 'tp')  4.93 us
    psum x1, blocking collectives, body(): lax.psum(denom.astype(jnp.bfloat16), 'tp').astype(jnp.float32)  4.93 us
  transfers between devices with their start and end apart: 3, of which 2 were waited for; matrix products, arithmetic and copies ran while one was open for 5% of the time, Pallas kernels for 0%

commit v1 on v0

--- a/solution.py
+++ b/solution.py
@@ -96,7 +96,7 @@
         preferred_element_type=jnp.float32,
     )
     mixed, denom = (
-        lax.psum(mixed.astype(jnp.bfloat16), "tp").astype(jnp.float32),
+        jnp.sum(lax.all_gather(mixed.astype(jnp.bfloat16), "tp"), axis=0).astype(jnp.float32),
         lax.psum(denom.astype(jnp.bfloat16), "tp").astype(jnp.float32),
     )
     att_out = (mixed / denom[:, :, None]).astype(jnp.bfloat16)

time: 123 us -> 110 us (0.89)
  waiting for transfers between devices: 32.8 us -> 16 us
  blocking collectives: 43.6 us -> 49.2 us
    psum x1 -> x0, waiting for transfers between devices: 16.8 us -> none  [body(): lax.psum(mixed.astype(jnp.bfloat16), 'tp').astype(jnp.float32)]
    all_gather x0 -> x1, blocking collectives: none -> 5.64 us  [body(): lax.all_gather(mixed.astype(jnp.bfloat16), 'tp')]
  transfers between devices with their start and end apart: 3 -> 2, of which waited for: 2 -> 1; matrix products, arithmetic and copies ran while one was open for 5% -> 5% of each run, Pallas kernels for 0% -> 0%
where the time goes in v1:
time: 110 us
  blocking collectives  49.2 us (45%)
  waiting for transfers between devices  16 us (15%)
  matrix products  15.1 us (14%)
  between operations  14.8 us (13%)
  local copies, waits for them, and re-layouts  5.8 us (5%)
  starting transfers between devices  5.69 us (5%)
  other arithmetic  3.19 us (3%)
    all_to_all x1, blocking collectives, body(): lax.all_to_all(packed, 'wide', split_axis=0, concat_axis=0, tiled=True)  20.4 us
    reduce_scatter x1, waiting for transfers between devices, body(): lax.psum_scatter(expert_part(flattened, gate_slice, up_slice, down_slice)...  16 us
    all_gather x1, blocking collectives, body(): column = lax.all_gather(arrived, ('tp', 'sub'), axis=0, tiled=True)  13.3 us
    all_to_all x1, starting transfers between devices, body(): lax.all_to_all(own_out, 'wide', split_axis=0, concat_axis=0, tiled=True)  5.65 us
    all_gather x1, blocking collectives, body(): lax.all_gather(mixed.astype(jnp.bfloat16), 'tp')  5.64 us
    dot_general x1, matrix products, expert_part(): jnp.dot(hidden, down_slice, preferred_element_type=jnp.float32)  5.4 us
    pmax x1, blocking collectives, body(): peak = lax.pmax(jnp.max(masked, axis=2), 'tp')  4.93 us
    psum x1, blocking collectives, body(): lax.psum(denom.astype(jnp.bfloat16), 'tp').astype(jnp.float32)  4.93 us
  transfers between devices with their start and end apart: 2, of which 1 were waited for; matrix products, arithmetic and copies ran while one was open for 5% of the time, Pallas kernels for 0%

profile of v1, /device:TPU:0, one launch (start us, length us, event | category | flops | bytes accessed | tf_op | source)
XLA Modules:
  0.0 109.8 jit_solution(14051981083115423527)
XLA Ops:
  7.2 0.0 copy-start
  7.2 0.0 reduce-scatter.2.cloned.1.call-start
  7.2 0.9 eq.36
  8.1 0.1 fusion.43
  8.2 0.1 reduce_window_sum.11
  8.3 0.2 select_reduce_fusion.1
  8.4 0.1 reduce_sum.69
  8.5 0.7 multiply_add_fusion
  9.2 1.1 fusion.22
  10.3 0.9 fusion.41
  11.2 0.1 multiply_divide_fusion
  11.2 0.1 convert_reduce_fusion
  11.3 1.1 convolution_convert_fusion.1
  12.4 0.1 reshape.163
  12.5 20.4 %all_to_all.10 = bf16[16,4,3584]{2,1,0:T(4,128)(2,1)S(1)} all-to-all(bf16[16,4,3584]{2,1,0:T(4,128)(2,1)S(1)} %reshape.163), channel_id=1, replica_groups=mesh['groups'=1,'wide'=16,'tp'=2,'sub'=1] {'wide'}, dimensions={0} | all-to-all | bytes 917504 | tf_op jit(solution)/shard_map/all_to_all | solution.py:62
  33.0 13.3 %all_gather.9 = bf16[32,4,3584]{2,1,0:T(4,128)(2,1)} all-gather(bf16[16,4,3584]{2,1,0:T(4,128)(2,1)S(1)} %all_to_all.10), channel_id=1, replica_groups=mesh['groups'=1,'wide'=16,'tp'=2,'sub'=1] {'tp','sub'}, dimensions={0}, use_global_device_ids=true | all-gather | bytes 1376256 | tf_op jit(solution)/shard_map/all_gather | solution.py:63
  46.3 1.7 %reshape.164 = bf16[128,3584]{1,0:T(8,128)(2,1)S(1)} reshape(bf16[32,4,3584]{2,1,0:T(4,128)(2,1)} %all_gather.9) | data formatting | bytes 1835008 | tf_op jit(solution)/shard_map/reshape | solution.py:64
  47.9 2.7 %fusion.3 = f32[128,512]{1,0:T(8,128)S(1)} fusion(bf16[128,3584]{1,0:T(8,128)(2,1)S(1)} %reshape.164, bf16[1,3584,512]{2,1,0:T(8,128)(2,1)} %param.14), kind=kOutput, calls=%fused_computation.6 | convolution fusion | flops 469762048 | bytes 4849664 | tf_op jit(solution)/shard_map/dot_general | solution.py:27
  50.6 0.0 copy-start.2
  50.6 5.4 %convolution_convert_fusion = bf16[128,3584]{1,0:T(8,128)(2,1)} fusion(bf16[1,512,3584]{2,1,0:T(8,128)(2,1)} %param.16, bf16[128,3584]{1,0:T(8,128)(2,1)S(1)} %reshape.164, bf16[1,3584,512]{2,1,0:T(8,128)(2,1)} %param.15, f32[128,512]{1,0:T(8,128)S(1)} %fusion.3), kind=kOutput, calls=%fused_computation | convolution fusion | flops 940376064 | bytes 9437184 | tf_op jit(solution)/shard_map/dot_general | solution.py:30
  56.0 0.0 copy-start.1
  56.0 0.0 reduce-scatter.2.cloned.1.call-update
  56.8 0.0 copy-done
  56.8 0.0 copy-done.2
  56.8 1.8 %fusion.9 = f32[128,2048]{1,0:T(8,128)} fusion(bf16[1,2048,512]{2,1,0:T(8,128)(2,1)S(1)} %copy-done, bf16[1,128,512]{2,1,0:T(8,128)(2,1)S(1)} %copy-done.2), kind=kOutput, calls=%fused_computation.13 | convolution fusion | flops 268435456 | bytes 3276800 | tf_op jit(solution)/shard_map/rhc,rlc->rhl/dot_general | solution.py:80
  58.6 16.0 %reduce-scatter.2.cloned.1.call-done = bf16[64,3584]{1,0:T(8,128)(2,1)} async-done(((bf16[128,3584]{1,0:T(8,128)(2,1)}), bf16[64,3584]{1,0:T(8,128)(2,1)}) %reduce-scatter.2.cloned.1.call-update) | async-done | bytes 458768 | tf_op jit(solution)/shard_map/reduce_scatter | solution.py:65
  74.5 1.9 %reshape.165 = bf16[16,4,3584]{2,1,0:T(4,128)(2,1)} reshape(bf16[64,3584]{1,0:T(8,128)(2,1)} %reduce-scatter.2.cloned.1.call-done) | data formatting | bytes 917504 | tf_op jit(solution)/shard_map/reshape | solution.py:73
  76.4 5.6 %all-to-all-start.1 = ((bf16[16,4,3584]{2,1,0:T(4,128)(2,1)}), bf16[16,4,3584]{2,1,0:T(4,128)(2,1)}, u32[]{:S(2)}, u32[]{:S(2)}) async-start(bf16[16,4,3584]{2,1,0:T(4,128)(2,1)} %reshape.165), calls=%async_computation.2 | async-start | bytes 917504 | tf_op jit(solution)/shard_map/all_to_all | solution.py:74
  82.1 0.0 copy-done.1
  82.1 1.7 %fusion.47 = (f32[128]{0:T(128)S(1)}, f32[128,2048]{1,0:T(8,128)S(1)}) fusion(f32[128,2048]{1,0:T(8,128)} %fusion.9, bf16[1,64,2048]{2,1,0:T(8,128)(2,1)S(1)} %copy-done.1, bf16[1,64,128]{2,1,0:T(8,128)(2,1)} %param.18, pred[2048]{0:T(1024)(128)(4,1)S(1)} %add_compare_fusion), kind=kOutput, calls=%fused_computation.55 | convolution fusion | flops 34602880 | bytes 2378240 | tf_op jit(solution)/shard_map/rkh,rkl->rhl/dot_general | solution.py:85
  83.8 4.9 %pmax.7 = f32[128]{0:T(128)S(1)} all-reduce(f32[128]{0:T(128)S(1)} %get-tuple-element.6), channel_id=1, replica_groups=mesh['groups'=1,'wide'=16,'tp'=2,'sub'=1] {'tp'}, use_global_device_ids=true, to_apply=%region_8.9 | all-reduce | flops 128 | bytes 1024 | tf_op jit(solution)/shard_map/pmax | solution.py:89
  88.7 0.3 fusion.25
  89.0 4.9 %psum.7 = bf16[128]{0:T(256)(128)(2,1)S(1)} all-reduce(bf16[128]{0:T(256)(128)(2,1)S(1)} %fusion.25), channel_id=1, replica_groups=mesh['groups'=1,'wide'=16,'tp'=2,'sub'=1] {'tp'}, use_global_device_ids=true, to_apply=%region_11.12 | all-reduce | flops 128 | bytes 512 | tf_op jit(solution)/shard_map/psum | solution.py:100
  94.0 0.5 fusion.17
  94.5 5.6 %all-gather = bf16[256,512]{1,0:T(8,128)(2,1)S(1)} all-gather(bf16[128,512]{1,0:T(8,128)(2,1)S(1)} %fusion.17), channel_id=2, replica_groups=mesh['groups'=1,'wide'=16,'tp'=2,'sub'=1] {'tp'}, dimensions={0}, use_global_device_ids=true | all-gather | bytes 393216 | tf_op jit(solution)/shard_map/all_gather | solution.py:99
  100.2 0.7 fusion.31
  100.9 0.0 all-to-all-done.1
  100.9 1.1 %reshape.166 = bf16[64,3584]{1,0:T(8,128)(2,1)S(1)} reshape(bf16[16,4,3584]{2,1,0:T(4,128)(2,1)} %all-to-all-done.1) | data formatting | bytes 917504 | tf_op jit(solution)/shard_map/reshape | solution.py:75
  102.0 0.9 convolution_convert_fusion.2
  (3 shorter events, 0.1 us)
Async XLA Ops:
  7.2 49.6 %copy-start = (bf16[1,2048,512]{2,1,0:T(8,128)(2,1)S(1)}, bf16[1,2048,512]{2,1,0:T(8,128)(2,1)}, u32[]{:S(2)}) copy-start(bf16[1,2048,512]{2,1,0:T(8,128)(2,1)} %param.19) | copy-start | bytes 6291460
  7.2 67.4 %reduce-scatter.2.cloned.1.call-start = ((), (), s32[]{:S(2)}) async-start(), calls=%async_computation.3 | async-start | bytes 1376256 | tf_op jit(solution)/shard_map/reduce_scatter | solution.py:65
  50.6 6.2 %copy-start.2 = (bf16[1,128,512]{2,1,0:T(8,128)(2,1)S(1)}, bf16[1,128,512]{2,1,0:T(8,128)(2,1)}, u32[]{:S(2)}) copy-start(bf16[1,128,512]{2,1,0:T(8,128)(2,1)} %param.17) | copy-start | bytes 393220
  56.0 26.1 %copy-start.1 = (bf16[1,64,2048]{2,1,0:T(8,128)(2,1)S(1)}, bf16[1,64,2048]{2,1,0:T(8,128)(2,1)}, u32[]{:S(2)}) copy-start(bf16[1,64,2048]{2,1,0:T(8,128)(2,1)} %param.20) | copy-start | bytes 786436
  76.4 24.5 %all-to-all-start.1 = ((bf16[16,4,3584]{2,1,0:T(4,128)(2,1)}), bf16[16,4,3584]{2,1,0:T(4,128)(2,1)}, u32[]{:S(2)}, u32[]{:S(2)}) async-start(bf16[16,4,3584]{2,1,0:T(4,128)(2,1)} %reshape.165), calls=%async_computation.2 | async-start | bytes 917504 | tf_op jit(solution)/shard_map/all_to_all | solution.py:74
Sparse Core Ops, SparseCore 0:
  56.2 18.3 reduce-scatter.1
